TPU v7x, 32 devices: a whole 2x2x4 slice. The times are simulated.
32 devices in a mesh: lat: 8 (over z, y), grp: 4 (over x, core).
Axes of the slice: x: 2, y: 2, z: 4, core: 2. Of those that a mesh axis runs over, the one named last changes fastest.
Arguments:
- tokens: bfloat16 [384, 64, 1024], P('grp', 'lat'), may hold values from -6 to 6
- cotangent: bfloat16 [384, 64, 1024], P('grp', 'lat'), may hold values from -6 to 6
- gain: float32 [384], P('grp'), may hold values from 0.5 to 1.5
- shift: float32 [384], P('grp'), may hold values from -3 to 3
- w_in: float32 [4, 2, 96, 96], P('grp'), may hold values from -0.4375 to 0.4375
- b_in: float32 [4, 2, 96], P('grp'), may hold values from -0.3 to 0.3
- w_out: float32 [4, 2, 96, 96], P('grp'), may hold values from -0.4375 to 0.4375
- b_out: float32 [4, 2, 96], P('grp'), may hold values from -0.12 to 0.12
Outputs:
- mixed: bfloat16 [384, 64, 1024], P('grp', 'lat')
- grad_tokens: bfloat16 [384, 64, 1024], P('grp', 'lat')
- grad_weights: float32 [4, 36864], P('grp', 'lat')
All inputs are finite; a program needn't handle non-finite values.
Results may differ from a plain program's by a relative error of at most 0.012.
Values sent between devices are 32-bit elements; how exact they have to be, the bound alone decides.
A program may use at most 128 MiB of HBM per device.

v0:
```python
import math
import jax
import jax.numpy as jnp
from jax import lax
from jax.sharding import PartitionSpec as P

highest = lax.Precision.HIGHEST
shrink_level = 0.01
norm_eps = 1e-05


def contract(form, left, right):
    return jnp.einsum(form, left, right, precision=highest)


def angle_table(left_count, right_count, length):
    left_index = jnp.arange(left_count, dtype=jnp.int32)[:, None]
    right_index = jnp.arange(right_count, dtype=jnp.int32)[None, :]
    phase = left_index * right_index % length
    theta = phase.astype(jnp.float32) * (2.0 * math.pi / length)
    return (jnp.cos(theta), jnp.sin(theta))


def lon_forward(field, modes):
    length = field.shape[2]
    cos_tab, sin_tab = angle_table(length, modes, length)
    scale = 1.0 / math.sqrt(length)
    out_real = contract("crn,nm->cmr", field, cos_tab) * scale
    out_imag = contract("crn,nm->cmr", field, sin_tab) * -scale
    return jnp.stack([out_real, out_imag])


def lon_inverse(stack, length, weighted):
    modes = stack.shape[2]
    cos_tab, sin_tab = angle_table(modes, length, length)
    scale = 1.0 / math.sqrt(length)
    real_part = stack[0]
    imag_part = stack[1]
    if weighted:
        mode_weight = jnp.where(jnp.arange(modes) == 0, 1.0, 2.0).astype(jnp.float32)[None, :, None]
        real_part = real_part * mode_weight
        imag_part = imag_part * mode_weight
    out = contract("cmr,mn->crn", real_part, cos_tab) - contract("cmr,mn->crn", imag_part, sin_tab)
    return out * scale


def lat_forward(stack):
    real_part, imag_part = (stack[0], stack[1])
    length = real_part.shape[-1]
    cos_tab, sin_tab = angle_table(length, length, length)
    scale = 1.0 / math.sqrt(length)
    out_real = contract("cql,lk->cqk", real_part, cos_tab) + contract(
        "cql,lk->cqk", imag_part, sin_tab
    )
    out_imag = contract("cql,lk->cqk", imag_part, cos_tab) - contract(
        "cql,lk->cqk", real_part, sin_tab
    )
    return (out_real * scale, out_imag * scale)


def lat_inverse(real_part, imag_part):
    length = real_part.shape[-1]
    cos_tab, sin_tab = angle_table(length, length, length)
    scale = 1.0 / math.sqrt(length)
    out_real = contract("cql,lk->cqk", real_part, cos_tab) - contract(
        "cql,lk->cqk", imag_part, sin_tab
    )
    out_imag = contract("cql,lk->cqk", imag_part, cos_tab) + contract(
        "cql,lk->cqk", real_part, sin_tab
    )
    return jnp.stack([out_real * scale, out_imag * scale])


def complex_mix(left_real, left_imag, weight):
    form = "bihk,bio->bohk"
    w_real = weight[:, 0]
    w_imag = weight[:, 1]
    out_real = contract(form, left_real, w_real) - contract(form, left_imag, w_imag)
    out_imag = contract(form, left_imag, w_real) + contract(form, left_real, w_imag)
    return (out_real, out_imag)


def mix_back(grad_real, grad_imag, weight):
    form = "bohk,bio->bihk"
    w_real = weight[:, 0]
    w_imag = weight[:, 1]
    back_real = contract(form, grad_real, w_real) + contract(form, grad_imag, w_imag)
    back_imag = contract(form, grad_imag, w_real) - contract(form, grad_real, w_imag)
    return (back_real, back_imag)


def weight_grad(left_real, left_imag, grad_real, grad_imag):
    form = "bihk,bohk->bio"
    grad_wreal = contract(form, left_real, grad_real) + contract(form, left_imag, grad_imag)
    grad_wimag = contract(form, left_real, grad_imag) - contract(form, left_imag, grad_real)
    return (grad_wreal, grad_wimag)


def shrink(value):
    return jnp.sign(value) * jnp.maximum(jnp.abs(value) - shrink_level, 0.0)


def regroup_modes(parts, lat_count, grp_count):
    _, two, chans, quarter, rows = parts.shape
    split = parts.reshape(lat_count, grp_count, two, chans, quarter, rows)
    split = jnp.transpose(split, (2, 1, 3, 4, 0, 5))
    return split.reshape(two, grp_count * chans, quarter, lat_count * rows)


def regroup_rows(stack, lat_count, grp_count, chans):
    two, _, quarter, lat_len = stack.shape
    rows = lat_len // lat_count
    split = stack.reshape(two, grp_count, chans, quarter, lat_count, rows)
    split = jnp.transpose(split, (4, 1, 0, 2, 3, 5))
    return split.reshape(lat_count * grp_count, two, chans, quarter, rows)


def per_device(tokens, cotangent, gain, shift, w_in, b_in, w_out, b_out):
    chans, rows, length = tokens.shape
    lat_count = lax.axis_size("lat")
    grp_count = lax.axis_size("grp")
    all_chans = chans * grp_count
    modes = length // 2
    tok_val = tokens.astype(jnp.float32)
    grad_val = cotangent.astype(jnp.float32)
    first_sum, second_sum = lax.psum(
        (jnp.sum(tok_val, axis=0), jnp.sum(tok_val * tok_val, axis=0)), "grp"
    )
    token_mean = first_sum / all_chans
    inv_std = lax.rsqrt(second_sum / all_chans - token_mean * token_mean + norm_eps)
    normed = (tok_val - token_mean) * inv_std
    normal_out = normed * gain[:, None, None] + shift[:, None, None]
    mode_weight = jnp.where(jnp.arange(modes) == 0, 1.0, 2.0).astype(jnp.float32)[
        None, None, :, None
    ]
    spec_field = lon_forward(normal_out, modes)
    spec_grad = lon_forward(grad_val, modes) * mode_weight
    parts_field, parts_grad = (
        lax.all_to_all(spec_field[None], ("lat", "grp"), split_axis=3, concat_axis=0, tiled=True),
        lax.all_to_all(spec_grad[None], ("lat", "grp"), split_axis=3, concat_axis=0, tiled=True),
    )
    modes_field = regroup_modes(parts_field, lat_count, grp_count)
    modes_grad = regroup_modes(parts_grad, lat_count, grp_count)
    block_in, bias_in, block_out, bias_out = (
        lax.all_gather(w_in, "grp", axis=0, tiled=True),
        lax.all_gather(b_in, "grp", axis=0, tiled=True),
        lax.all_gather(w_out, "grp", axis=0, tiled=True),
        lax.all_gather(b_out, "grp", axis=0, tiled=True),
    )
    block_count = block_in.shape[0]
    block_size = block_in.shape[2]
    quarter = modes_field.shape[2]
    lat_len = modes_field.shape[3]
    spec_real, spec_imag = lat_forward(modes_field)
    grad_real, grad_imag = lat_forward(modes_grad)
    blocked = (block_count, block_size, quarter, lat_len)
    spec_real = spec_real.reshape(blocked)
    spec_imag = spec_imag.reshape(blocked)
    grad_real = grad_real.reshape(blocked)
    grad_imag = grad_imag.reshape(blocked)
    pre_real, pre_imag = complex_mix(spec_real, spec_imag, block_in)
    pre_real = pre_real + bias_in[:, 0, :, None, None]
    pre_imag = pre_imag + bias_in[:, 1, :, None, None]
    act_real = jax.nn.relu(pre_real)
    act_imag = jax.nn.relu(pre_imag)
    post_real, post_imag = complex_mix(act_real, act_imag, block_out)
    post_real = post_real + bias_out[:, 0, :, None, None]
    post_imag = post_imag + bias_out[:, 1, :, None, None]
    shrunk_real = shrink(post_real)
    shrunk_imag = shrink(post_imag)
    d_post_real = jnp.where(jnp.abs(post_real) > shrink_level, grad_real, 0.0)
    d_post_imag = jnp.where(jnp.abs(post_imag) > shrink_level, grad_imag, 0.0)
    g_out_real, g_out_imag = weight_grad(act_real, act_imag, d_post_real, d_post_imag)
    d_act_real, d_act_imag = mix_back(d_post_real, d_post_imag, block_out)
    d_pre_real = jnp.where(pre_real > 0.0, d_act_real, 0.0)
    d_pre_imag = jnp.where(pre_imag > 0.0, d_act_imag, 0.0)
    g_in_real, g_in_imag = weight_grad(spec_real, spec_imag, d_pre_real, d_pre_imag)
    d_spec_real, d_spec_imag = mix_back(d_pre_real, d_pre_imag, block_in)
    flat_shape = (block_count * block_size, quarter, lat_len)
    back_field = lat_inverse(shrunk_real.reshape(flat_shape), shrunk_imag.reshape(flat_shape))
    back_grad = lat_inverse(d_spec_real.reshape(flat_shape), d_spec_imag.reshape(flat_shape))
    grad_stack = jnp.stack([g_in_real, g_in_imag, g_out_real, g_out_imag], axis=1)
    grad_term = grad_stack.reshape(block_count, 4 * block_size * block_size) * (
        1.0 / math.sqrt(lat_len * modes)
    )
    send_field = regroup_rows(back_field, lat_count, grp_count, chans)
    send_grad = regroup_rows(back_grad, lat_count, grp_count, chans)
    rows_field, rows_grad = (
        lax.all_to_all(send_field, ("lat", "grp"), split_axis=0, concat_axis=3, tiled=True),
        lax.all_to_all(send_grad, ("lat", "grp"), split_axis=0, concat_axis=3, tiled=True),
    )
    rows_field = rows_field[0]
    rows_grad = rows_grad[0]
    piece = grad_term.shape[1] // lat_count
    ordered = jnp.transpose(grad_term.reshape(block_count, lat_count, piece), (1, 0, 2))
    grad_weights = lax.psum_scatter(
        ordered.reshape(lat_count * block_count, piece),
        ("lat", "grp"),
        scatter_dimension=0,
        tiled=True,
    )
    filtered = lon_inverse(rows_field, length, True)
    pulled = lon_inverse(rows_grad, length, False)
    mixed = (filtered + normal_out + tok_val).astype(jnp.bfloat16)
    d_normal = grad_val + pulled
    dnorm = d_normal * gain[:, None, None]
    back_one, back_two = lax.psum((jnp.sum(dnorm, axis=0), jnp.sum(dnorm * normed, axis=0)), "grp")
    grad_tokens = grad_val + inv_std * (
        dnorm - back_one / all_chans - normed * (back_two / all_chans)
    )
    return (mixed, grad_tokens.astype(jnp.bfloat16), grad_weights)


def solution(mesh):
    in_specs = (
        P("grp", "lat", None),
        P("grp", "lat", None),
        P("grp"),
        P("grp"),
        P("grp", None, None, None),
        P("grp", None, None),
        P("grp", None, None, None),
        P("grp", None, None),
    )
    out_specs = (P("grp", "lat", None), P("grp", "lat", None), P("grp", "lat"))
    return jax.shard_map(
        per_device, mesh=mesh, in_specs=in_specs, out_specs=out_specs, check_vma=False
    )
```

profile of v0, /device:TPU:0, one launch (start us, length us, event | category | flops | bytes accessed | tf_op | source)
XLA Modules:
  0.0 715.0 jit_solution(96283752565888602)
XLA Ops:
  7.2 12.5 %multiply_bitcast_fusion.2 = f32[1,1,96,512,8]{3,2,4,1,0:T(8,128)S(1)} fusion(bf16[96,8,1024]{2,1,0:T(8,128)(2,1)} %param.9), kind=kOutput, calls=%fused_computation.130 | convolution fusion | flops 4839571456 | bytes 3145728 | tf_op jit(solution)/shard_map/crn,nm->cmr/dot_general | solution.py:13
  19.7 11.4 %multiply_bitcast_fusion.3 = f32[1,1,96,512,8]{3,2,4,1,0:T(8,128)S(1)} fusion(bf16[96,8,1024]{2,1,0:T(8,128)(2,1)S(1)} %copy-done.30), kind=kOutput, calls=%fused_computation.131 | convolution fusion | flops 4839571456 | bytes 3145728 | tf_op jit(solution)/shard_map/crn,nm->cmr/dot_general | solution.py:13
  35.1 7.5 %all-to-all-start.2 = ((f32[1,2,96,512,8]{2,4,1,0,3:T(8,128)}), f32[1,2,96,512,8]{2,4,1,0,3:T(8,128)}, u32[]{:S(2)}, u32[]{:S(2)}) async-start(f32[1,2,96,512,8]{2,4,1,0,3:T(8,128)} %copy.115), calls=%async_computation.2 | async-start | bytes 8388608 | tf_op jit(solution)/shard_map/all_to_all | solution.py:140
  43.9 41.2 %all-reduce.11.cloned.1.call-done = (f32[8,1024]{1,0:T(8,128)}, f32[8,1024]{1,0:T(8,128)}) async-done(((f32[8,1024]{1,0:T(8,128)}, f32[8,1024]{1,0:T(8,128)}), (f32[8,1024]{1,0:T(8,128)}, f32[8,1024]{1,0:T(8,128)})) %all-reduce.11.cloned.1.call-update) | async-done | bytes 65552 | tf_op jit(solution)/shard_map/psum | solution.py:126
  87.0 14.2 %multiply_bitcast_fusion.4 = f32[1,96,512,8]{2,1,3,0:T(8,128)S(1)} fusion(f32[96,8,1024]{2,1,0:T(8,128)S(1)} %fusion.6), kind=kOutput, calls=%fused_computation.136 | convolution fusion | flops 4839571456 | bytes 4718592 | tf_op jit(solution)/shard_map/crn,nm->cmr/dot_general | solution.py:13
  101.2 13.8 %multiply_bitcast_fusion.5 = f32[1,96,512,8]{2,1,3,0:T(8,128)S(1)} fusion(f32[96,8,1024]{2,1,0:T(8,128)S(1)} %fusion.6), kind=kOutput, calls=%fused_computation.137 | convolution fusion | flops 4839571456 | bytes 4718592 | tf_op jit(solution)/shard_map/crn,nm->cmr/dot_general | solution.py:13
  118.9 17.3 %all-to-all-done.2 = f32[1,2,96,512,8]{2,4,1,0,3:T(8,128)} async-done(((f32[1,2,96,512,8]{2,4,1,0,3:T(8,128)}), f32[1,2,96,512,8]{2,4,1,0,3:T(8,128)}, u32[]{:S(2)}, u32[]{:S(2)}) %all-to-all-start.2) | async-done | bytes 3145760 | tf_op jit(solution)/shard_map/all_to_all | solution.py:140
  136.2 4.2 all-to-all-start
  140.5 27.9 %all_gather.13 = f32[4,2,96]{2,1,0:T(2,128)S(1)} all-gather(f32[1,2,96]{2,1,0:T(2,128)S(1)} %copy-done.39), channel_id=1, replica_groups=mesh['lat'=8,'grp'=4] {'grp'}, dimensions={0}, use_global_device_ids=true | all-gather | bytes 3840 | tf_op jit(solution)/shard_map/all_gather | solution.py:146
  168.4 5.7 all_gather.15
  174.1 6.7 all_gather.12
  180.7 13.8 %all_gather.14 = f32[4,2,96,96]{3,2,0,1:T(8,128)} all-gather(f32[1,2,96,96]{3,2,0,1:T(8,128)S(1)} %bitcast.375), channel_id=1, replica_groups=mesh['lat'=8,'grp'=4] {'grp'}, dimensions={0}, use_global_device_ids=true | all-gather | bytes 368640 | tf_op jit(solution)/shard_map/all_gather | solution.py:147
  195.2 4.9 copy.198
  221.7 12.5 %all-to-all-done = f32[1,2,96,512,8]{2,4,1,0,3:T(8,128)} async-done(((f32[1,2,96,512,8]{2,4,1,0,3:T(8,128)}), f32[1,2,96,512,8]{2,4,1,0,3:T(8,128)}, u32[]{:S(2)}, u32[]{:S(2)}) %all-to-all-start) | async-done | bytes 3145760 | tf_op jit(solution)/shard_map/all_to_all | solution.py:139
  234.2 4.9 copy.199
  274.3 3.8 copy_select_fusion
  284.8 6.5 copy_select_fusion.1
  323.7 4.4 all-to-all-start.1
  328.2 3.7 fusion.208
  350.2 3.7 fusion.28
  387.7 34.0 %all-to-all-done.1 = f32[32,2,96,16,8]{2,4,3,1,0:T(8,128)} async-done(((f32[32,2,96,16,8]{2,4,3,1,0:T(8,128)}), f32[32,2,96,16,8]{2,4,3,1,0:T(8,128)}, u32[]{:S(2)}, u32[]{:S(2)}) %all-to-all-start.1) | async-done | bytes 3145760 | tf_op jit(solution)/shard_map/all_to_all | solution.py:189
  421.7 4.2 all-to-all-start.3
  426.2 5.8 fusion.127
  439.0 3.8 fusion.141
  459.0 143.5 %all-reduce.7.cloned.1.call-done = f32[32,4608]{1,0:T(8,128)} async-done(((f32[32,4608]{1,0:T(8,128)}), f32[32,4608]{1,0:T(8,128)}) %all-reduce.7.cloned.1.call-update) | async-done | bytes 589840
  614.1 15.6 %fusion.40 = f32[96,8,1024]{2,1,0:T(8,128)} fusion(f32[96,512,8]{1,2,0:T(8,128)} %copy.112), kind=kOutput, calls=%fused_computation.58 | convolution fusion | flops 4839178240 | bytes 4718592 | tf_op jit(solution)/shard_map/cmr,mn->crn/dot_general | solution.py:13
  629.6 3.9 fusion.364
  638.5 16.3 %fusion.38 = f32[96,8,1024]{2,1,0:T(8,128)S(1)} fusion(f32[96,512,8]{1,2,0:T(8,128)} %copy.125), kind=kOutput, calls=%fused_computation.56 | convolution fusion | flops 4839178240 | bytes 4718592 | tf_op jit(solution)/shard_map/cmr,mn->crn/dot_general | solution.py:13
  654.8 15.9 %fusion.363 = (f32[8,1024]{1,0:T(8,128)}, f32[8,1024]{1,0:T(8,128)}, f32[96,8,1024]{2,1,0:T(8,128)}) fusion(f32[8,1024]{1,0:T(8,128)S(1)} %copy-done.35, f32[8,1024]{1,0:T(8,128)S(1)} %copy-done.33, bf16[96,8,1024]{2,1,0:T(8,128)(2,1)S(1)} %copy-done.23, f32[96]{0:T(128)S(1)} %copy-done.44, f32[96,8,1024]{2,1,0:T(8,128)S(1)} %fusion.38, ...), kind=kOutput, calls=%fused_computation.321 | convolution fusion | flops 4847812608 | bytes 11141504 | tf_op jit(solution)/shard_map/cmr,mn->crn/dot_general | solution.py:13
  670.8 16.3 %fusion.11 = bf16[96,8,1024]{2,1,0:T(8,128)(2,1)} fusion(bf16[96,8,1024]{2,1,0:T(8,128)(2,1)S(1)} %copy-done.23, f32[96,8,1024]{2,1,0:T(8,128)} %fusion.40, f32[96,512,8]{1,2,0:T(8,128)S(1)} %copy-done.28, f32[96]{0:T(128)S(1)} %copy-done.42, f32[96]{0:T(128)S(1)} %copy-done.44, f32[8,1024]{1,0:T(8,128)S(1)} %copy-done.35, f32[8,1024]{1,0:T(8,128)S(1)} %copy-done.33), kind=kOutput, calls=%fused_computation.21 | convolution fusion | flops 4847042560 | bytes 7930624 | tf_op jit(solution)/shard_map/cmr,mn->crn/dot_general | solution.py:13
  687.0 15.7 %all-reduce.9.cloned.1.call-done = (f32[8,1024]{1,0:T(8,128)}, f32[8,1024]{1,0:T(8,128)}) async-done(((f32[8,1024]{1,0:T(8,128)}, f32[8,1024]{1,0:T(8,128)}), (f32[8,1024]{1,0:T(8,128)}, f32[8,1024]{1,0:T(8,128)})) %all-reduce.9.cloned.1.call-update) | async-done | bytes 65552 | tf_op jit(solution)/shard_map/psum | solution.py:207
  703.5 4.5 fusion.1
  (184 shorter events, 199.7 us)
Async XLA Ops:
  7.2 12.5 %copy-start.30 = (bf16[96,8,1024]{2,1,0:T(8,128)(2,1)S(1)}, bf16[96,8,1024]{2,1,0:T(8,128)(2,1)}, u32[]{:S(2)}) copy-start(bf16[96,8,1024]{2,1,0:T(8,128)(2,1)} %param.9) | copy-start | bytes 4718596
  35.1 7.7 %copy-start.22 = (bf16[96,8,1024]{2,1,0:T(8,128)(2,1)S(1)}, bf16[96,8,1024]{2,1,0:T(8,128)(2,1)}, u32[]{:S(2)}) copy-start(bf16[96,8,1024]{2,1,0:T(8,128)(2,1)} %param.8) | copy-start | bytes 4718596
  35.1 51.4 %copy-start.41 = (f32[96]{0:T(128)S(1)}, f32[96]{0:T(128)}, u32[]{:S(2)}) copy-start(f32[96]{0:T(128)} %param.11) | copy-start | bytes 1156
  35.1 51.4 %copy-start.43 = (f32[96]{0:T(128)S(1)}, f32[96]{0:T(128)}, u32[]{:S(2)}) copy-start(f32[96]{0:T(128)} %param.10) | copy-start | bytes 1156
  35.1 101.2 %all-to-all-start.2 = ((f32[1,2,96,512,8]{2,4,1,0,3:T(8,128)}), f32[1,2,96,512,8]{2,4,1,0,3:T(8,128)}, u32[]{:S(2)}, u32[]{:S(2)}) async-start(f32[1,2,96,512,8]{2,4,1,0,3:T(8,128)} %copy.115), calls=%async_computation.2 | async-start | bytes 8388608 | tf_op jit(solution)/shard_map/all_to_all | solution.py:140
  42.5 42.5 %all-reduce.11.cloned.1.call-start = ((), (), s32[]{:S(2)}) async-start(), calls=%async_computation.6 | async-start | bytes 131072 | tf_op jit(solution)/shard_map/psum | solution.py:126
  118.9 21.6 %copy-start.39 = (f32[1,2,96]{2,1,0:T(2,128)S(1)}, f32[1,2,96]{2,1,0:T(2,128)}, u32[]{:S(2)}) copy-start(f32[1,2,96]{2,1,0:T(2,128)} %param.13) | copy-start | bytes 2308
  118.9 49.5 %copy-start.40 = (f32[1,2,96]{2,1,0:T(2,128)S(1)}, f32[1,2,96]{2,1,0:T(2,128)}, u32[]{:S(2)}) copy-start(f32[1,2,96]{2,1,0:T(2,128)} %param.15) | copy-start | bytes 2308
  118.9 55.2 %copy-start.36 = (f32[1,2,96,96]{3,2,1,0:T(8,128)S(1)}, f32[1,2,96,96]{3,2,1,0:T(8,128)}, u32[]{:S(2)}) copy-start(f32[1,2,96,96]{3,2,1,0:T(8,128)} %param.12) | copy-start | bytes 221188
  118.9 61.8 %copy-start.37 = (f32[1,2,96,96]{3,2,1,0:T(8,128)S(1)}, f32[1,2,96,96]{3,2,1,0:T(8,128)}, u32[]{:S(2)}) copy-start(f32[1,2,96,96]{3,2,1,0:T(8,128)} %param.14) | copy-start | bytes 221188
  136.2 97.9 %all-to-all-start = ((f32[1,2,96,512,8]{2,4,1,0,3:T(8,128)}), f32[1,2,96,512,8]{2,4,1,0,3:T(8,128)}, u32[]{:S(2)}, u32[]{:S(2)}) async-start(f32[1,2,96,512,8]{2,4,1,0,3:T(8,128)} %copy.98), calls=%async_computation | async-start | bytes 8388608 | tf_op jit(solution)/shard_map/all_to_all | solution.py:139
  274.3 3.8 copy-start
  323.7 98.0 %all-to-all-start.1 = ((f32[32,2,96,16,8]{2,4,3,1,0:T(8,128)}), f32[32,2,96,16,8]{2,4,3,1,0:T(8,128)}, u32[]{:S(2)}, u32[]{:S(2)}) async-start(f32[32,2,96,16,8]{2,4,3,1,0:T(8,128)} %bitcast.368), calls=%async_computation.1 | async-start | bytes 8388608 | tf_op jit(solution)/shard_map/all_to_all | solution.py:189
  328.2 3.7 copy-start.15
  350.2 3.7 copy-start.9
  421.7 208.0 %all-to-all-start.3 = ((f32[32,2,96,16,8]{2,4,3,1,0:T(8,128)}), f32[32,2,96,16,8]{2,4,3,1,0:T(8,128)}, u32[]{:S(2)}, u32[]{:S(2)}) async-start(f32[32,2,96,16,8]{2,4,3,1,0:T(8,128)} %bitcast.367), calls=%async_computation.3 | async-start | bytes 8388608 | tf_op jit(solution)/shard_map/all_to_all | solution.py:190
  425.9 176.5 %all-reduce.7.cloned.1.call-start = ((), (), s32[]{:S(2)}) async-start(), calls=%async_computation.4 | async-start | bytes 1179648
  426.2 5.9 copy-start.2
  426.2 5.9 copy-start.16
  432.0 3.5 copy-start.4
  432.1 3.5 copy-start.10
  442.9 3.5 copy-start.14
  446.4 3.5 copy-start.12
  458.9 243.8 %all-reduce.9.cloned.1.call-start = ((), (), s32[]{:S(2)}) async-start(), calls=%async_computation.5 | async-start | bytes 131072 | tf_op jit(solution)/shard_map/psum | solution.py:207
  638.4 16.3 %copy-start.23 = (bf16[96,8,1024]{2,1,0:T(8,128)(2,1)S(1)}, bf16[96,8,1024]{2,1,0:T(8,128)(2,1)}, u32[]{:S(2)}) copy-start(bf16[96,8,1024]{2,1,0:T(8,128)(2,1)} %param.8) | copy-start | bytes 4718596
  638.4 16.3 %copy-start.29 = (f32[96,512,8]{1,2,0:T(8,128)S(1)}, f32[96,512,8]{1,2,0:T(8,128)}, u32[]{:S(2)}) copy-start(f32[96,512,8]{1,2,0:T(8,128)} %copy.124) | copy-start | bytes 4718596
  638.4 16.3 %copy-start.31 = (bf16[96,8,1024]{2,1,0:T(8,128)(2,1)S(1)}, bf16[96,8,1024]{2,1,0:T(8,128)(2,1)}, u32[]{:S(2)}) copy-start(bf16[96,8,1024]{2,1,0:T(8,128)(2,1)} %param.9) | copy-start | bytes 4718596
  638.4 16.4 %copy-start.33 = (f32[8,1024]{1,0:T(8,128)S(1)}, f32[8,1024]{1,0:T(8,128)}, u32[]{:S(2)}) copy-start(f32[8,1024]{1,0:T(8,128)} %copy-done.32) | copy-start | bytes 98308
  638.4 16.4 %copy-start.35 = (f32[8,1024]{1,0:T(8,128)S(1)}, f32[8,1024]{1,0:T(8,128)}, u32[]{:S(2)}) copy-start(f32[8,1024]{1,0:T(8,128)} %copy-done.34) | copy-start | bytes 98308
  638.5 16.4 %copy-start.44 = (f32[96]{0:T(128)S(1)}, f32[96]{0:T(128)}, u32[]{:S(2)}) copy-start(f32[96]{0:T(128)} %param.10) | copy-start | bytes 1156
  654.8 15.9 %copy-start.28 = (f32[96,512,8]{1,2,0:T(8,128)S(1)}, f32[96,512,8]{1,2,0:T(8,128)}, u32[]{:S(2)}) copy-start(f32[96,512,8]{1,2,0:T(8,128)} %copy.111) | copy-start | bytes 4718596
  654.8 15.9 %copy-start.42 = (f32[96]{0:T(128)S(1)}, f32[96]{0:T(128)}, u32[]{:S(2)}) copy-start(f32[96]{0:T(128)} %param.11) | copy-start | bytes 1156
  (20 other events, 45.7 us)
Sparse Core Ops, SparseCore 0:
  46.3 38.6 all-reduce.10
  459.1 143.3 all-reduce.6
  670.9 31.8 all-reduce.8
where the time goes:
time: 725 us; the launch traced here: 715 us
  waiting for transfers between devices  264 us (36%)
  matrix products  227 us (31%)
  local copies, waits for them, and re-layouts  116 us (16%)
  blocking collectives  54.1 us (7%)
  starting transfers between devices  20.8 us (3%)
  other arithmetic  17.5 us (2%)
  between operations  15.1 us (2%)
    dot_general x48, matrix products, contract(): return jnp.einsum(form, left, right, precision=highest)  227 us
    unnamed x4, waiting for transfers between devices  144 us
    psum x1, waiting for transfers between devices, per_device(): lax.psum((jnp.sum(tok_val, axis=0), jnp.sum(tok_val * tok_val, axis=0)),...  41.2 us
    all_to_all x1, waiting for transfers between devices, per_device(): lax.all_to_all(send_field, ('lat', 'grp'), split_axis=0, concat_axis=3, t...  34 us
    all_gather x1, blocking collectives, per_device(): lax.all_gather(b_in, 'grp', axis=0, tiled=True)  27.9 us
    another operation x8, local copies, waits for them, and re-layouts, lat_inverse(): return jnp.stack([out_real * scale, out_imag * scale])  24.5 us
    all_to_all x1, waiting for transfers between devices, per_device(): lax.all_to_all(spec_grad[None], ('lat', 'grp'), split_axis=3, concat_axis...  17.3 us
    psum x1, waiting for transfers between devices, per_device(): lax.psum((jnp.sum(dnorm, axis=0), jnp.sum(dnorm * normed, axis=0)), 'grp')  15.7 us
  transfers between devices with their start and end apart: 7, of which 6 were waited for; matrix products, arithmetic and copies ran while one was open for 27% of the time, Pallas kernels for 0%

commit v1 on v0

--- a/solution.py
+++ b/solution.py
@@ -7,6 +7,12 @@
 highest = lax.Precision.HIGHEST
 shrink_level = 0.01
 norm_eps = 1e-05
+
+
+def exchange_blocks(block, axis, split, join):
+    parts = jnp.split(block, lax.axis_size(axis), axis=split)
+    arrived = lax.all_to_all(jnp.stack(parts), axis, 0, 0)
+    return jnp.concatenate(arrived, axis=join)
 
 
 def contract(form, left, right):
@@ -186,7 +192,7 @@
     send_field = regroup_rows(back_field, lat_count, grp_count, chans)
     send_grad = regroup_rows(back_grad, lat_count, grp_count, chans)
     rows_field, rows_grad = (
-        lax.all_to_all(send_field, ("lat", "grp"), split_axis=0, concat_axis=3, tiled=True),
+        exchange_blocks(send_field, ("lat", "grp"), 0, 3),
         lax.all_to_all(send_grad, ("lat", "grp"), split_axis=0, concat_axis=3, tiled=True),
     )
     rows_field = rows_field[0]

time: 725 us -> 783 us (1.080)
  waiting for transfers between devices: 264 us -> 300 us
  local copies, waits for them, and re-layouts: 116 us -> 138 us
    all_to_all x1, waiting for transfers between devices: 0.01 us -> 70 us  [per_device(): lax.all_to_all(send_grad, ('lat', 'grp'), split_axis=0, concat_axis=3, ti...]
    all_to_all x1, waiting for transfers between devices: 34 us -> 0.01 us  [exchange_blocks(): arrived = lax.all_to_all(jnp.stack(parts), axis, 0, 0)]
    unnamed x91 -> x126, local copies, waits for them, and re-layouts: 4.63 us -> 23.7 us
  transfers between devices with their start and end apart: 7 -> 7, of which waited for: 6 -> 6; matrix products, arithmetic and copies ran while one was open for 27% -> 21% of each run, Pallas kernels for 0% -> 0%
where the time goes in v1:
time: 783 us; the launch traced here: 773 us
  waiting for transfers between devices  300 us (38%)
  matrix products  226 us (29%)
  local copies, waits for them, and re-layouts  138 us (18%)
  blocking collectives  54.1 us (7%)
  starting transfers between devices  20.6 us (3%)
  other arithmetic  19.3 us (2%)
  between operations  15.1 us (2%)
    dot_general x48, matrix products, contract(): return jnp.einsum(form, left, right, precision=highest)  226 us
    unnamed x4, waiting for transfers between devices  143 us
    all_to_all x1, waiting for transfers between devices, per_device(): lax.all_to_all(send_grad, ('lat', 'grp'), split_axis=0, concat_axis=3, ti...  70 us
    psum x1, waiting for transfers between devices, per_device(): lax.psum((jnp.sum(tok_val, axis=0), jnp.sum(tok_val * tok_val, axis=0)),...  41.2 us
    all_gather x1, blocking collectives, per_device(): lax.all_gather(b_in, 'grp', axis=0, tiled=True)  27.9 us
    another operation x8, local copies, waits for them, and re-layouts, lat_inverse(): return jnp.stack([out_real * scale, out_imag * scale])  25.9 us
    unnamed x126, local copies, waits for them, and re-layouts  23.7 us
    all_to_all x1, waiting for transfers between devices, per_device(): lax.all_to_all(spec_grad[None], ('lat', 'grp'), split_axis=3, concat_axis...  17.3 us
  transfers between devices with their start and end apart: 7, of which 6 were waited for; matrix products, arithmetic and copies ran while one was open for 21% of the time, Pallas kernels for 0%

profile of v1, /device:TPU:0, one launch (start us, length us, event | category | flops | bytes accessed | tf_op | source)
XLA Modules:
  0.0 773.2 jit_solution(6496265243863393427)
XLA Ops:
  7.2 12.5 %multiply_bitcast_fusion.2 = f32[1,1,96,512,8]{3,2,4,1,0:T(8,128)S(1)} fusion(bf16[96,8,1024]{2,1,0:T(8,128)(2,1)} %param.9), kind=kOutput, calls=%fused_computation.130 | convolution fusion | flops 4839571456 | bytes 3145728 | tf_op jit(solution)/shard_map/crn,nm->cmr/dot_general | solution.py:19
  19.7 11.4 %multiply_bitcast_fusion.3 = f32[1,1,96,512,8]{3,2,4,1,0:T(8,128)S(1)} fusion(bf16[96,8,1024]{2,1,0:T(8,128)(2,1)S(1)} %copy-done.31), kind=kOutput, calls=%fused_computation.131 | convolution fusion | flops 4839571456 | bytes 3145728 | tf_op jit(solution)/shard_map/crn,nm->cmr/dot_general | solution.py:19
  35.1 7.5 all-to-all-start.2
  43.9 41.2 %all-reduce.11.cloned.1.call-done = (f32[8,1024]{1,0:T(8,128)}, f32[8,1024]{1,0:T(8,128)}) async-done(((f32[8,1024]{1,0:T(8,128)}, f32[8,1024]{1,0:T(8,128)}), (f32[8,1024]{1,0:T(8,128)}, f32[8,1024]{1,0:T(8,128)})) %all-reduce.11.cloned.1.call-update) | async-done | bytes 65552 | tf_op jit(solution)/shard_map/psum | solution.py:132
  87.0 14.2 %multiply_bitcast_fusion.4 = f32[1,96,512,8]{2,1,3,0:T(8,128)S(1)} fusion(f32[96,8,1024]{2,1,0:T(8,128)S(1)} %fusion.6), kind=kOutput, calls=%fused_computation.136 | convolution fusion | flops 4839571456 | bytes 4718592 | tf_op jit(solution)/shard_map/crn,nm->cmr/dot_general | solution.py:19
  101.2 13.8 %multiply_bitcast_fusion.5 = f32[1,96,512,8]{2,1,3,0:T(8,128)S(1)} fusion(f32[96,8,1024]{2,1,0:T(8,128)S(1)} %fusion.6), kind=kOutput, calls=%fused_computation.137 | convolution fusion | flops 4839571456 | bytes 4718592 | tf_op jit(solution)/shard_map/crn,nm->cmr/dot_general | solution.py:19
  119.0 17.3 %all-to-all-done.2 = f32[1,2,96,512,8]{2,4,1,0,3:T(8,128)} async-done(((f32[1,2,96,512,8]{2,4,1,0,3:T(8,128)}), f32[1,2,96,512,8]{2,4,1,0,3:T(8,128)}, u32[]{:S(2)}, u32[]{:S(2)}) %all-to-all-start.2) | async-done | bytes 3145760 | tf_op jit(solution)/shard_map/all_to_all | solution.py:146
  136.2 4.2 all-to-all-start
  140.5 27.9 %all_gather.13 = f32[4,2,96]{2,1,0:T(2,128)S(1)} all-gather(f32[1,2,96]{2,1,0:T(2,128)S(1)} %copy-done.40), channel_id=1, replica_groups=mesh['lat'=8,'grp'=4] {'grp'}, dimensions={0}, use_global_device_ids=true | all-gather | bytes 3840 | tf_op jit(solution)/shard_map/all_gather | solution.py:152
  168.4 5.7 all_gather.15
  174.1 6.7 all_gather.12
  180.7 13.8 %all_gather.14 = f32[4,2,96,96]{3,2,0,1:T(8,128)} all-gather(f32[1,2,96,96]{3,2,0,1:T(8,128)S(1)} %bitcast.532), channel_id=1, replica_groups=mesh['lat'=8,'grp'=4] {'grp'}, dimensions={0}, use_global_device_ids=true | all-gather | bytes 368640 | tf_op jit(solution)/shard_map/all_gather | solution.py:153
  195.2 4.9 copy.229
  221.7 12.5 %all-to-all-done = f32[1,2,96,512,8]{2,4,1,0,3:T(8,128)} async-done(((f32[1,2,96,512,8]{2,4,1,0,3:T(8,128)}), f32[1,2,96,512,8]{2,4,1,0,3:T(8,128)}, u32[]{:S(2)}, u32[]{:S(2)}) %all-to-all-start) | async-done | bytes 3145760 | tf_op jit(solution)/shard_map/all_to_all | solution.py:145
  234.2 4.9 copy.230
  277.9 3.9 copy_select_fusion.1
  287.3 3.7 fusion.26
  333.8 4.0 add_select_fusion.2
  349.3 4.3 copy.151
  382.5 4.2 all-to-all-start.3
  410.5 70.0 %all-to-all-done.3 = f32[32,2,96,16,8]{2,4,3,1,0:T(8,128)} async-done(((f32[32,2,96,16,8]{2,4,3,1,0:T(8,128)}), f32[32,2,96,16,8]{2,4,3,1,0:T(8,128)}, u32[]{:S(2)}, u32[]{:S(2)}) %all-to-all-start.3) | async-done | bytes 3145760 | tf_op jit(solution)/shard_map/all_to_all | solution.py:196
  480.5 4.2 all-to-all-start.1
  485.0 5.8 fusion.127
  497.8 3.8 fusion.141
  517.8 143.4 %all-reduce.7.cloned.1.call-done = f32[32,4608]{1,0:T(8,128)} async-done(((f32[32,4608]{1,0:T(8,128)}), f32[32,4608]{1,0:T(8,128)}) %all-reduce.7.cloned.1.call-update) | async-done | bytes 589840
  662.7 3.9 fusion.396
  671.5 15.6 %fusion.38 = f32[96,8,1024]{2,1,0:T(8,128)} fusion(f32[96,512,8]{1,2,0:T(8,128)} %copy.156), kind=kOutput, calls=%fused_computation.56 | convolution fusion | flops 4839178240 | bytes 4718592 | tf_op jit(solution)/shard_map/cmr,mn->crn/dot_general | solution.py:19
  697.2 15.7 %fusion.40 = f32[96,8,1024]{2,1,0:T(8,128)} fusion(f32[96,512,8]{1,2,0:T(8,128)} %copy.143), kind=kOutput, calls=%fused_computation.58 | convolution fusion | flops 4839178240 | bytes 4718592 | tf_op jit(solution)/shard_map/cmr,mn->crn/dot_general | solution.py:19
  713.0 15.9 %fusion.395 = (f32[8,1024]{1,0:T(8,128)}, f32[8,1024]{1,0:T(8,128)}, f32[96,8,1024]{2,1,0:T(8,128)}) fusion(f32[8,1024]{1,0:T(8,128)S(1)} %copy-done.36, f32[8,1024]{1,0:T(8,128)S(1)} %copy-done.34, bf16[96,8,1024]{2,1,0:T(8,128)(2,1)S(1)} %copy-done.22, f32[96]{0:T(128)S(1)} %copy-done.45, f32[96,8,1024]{2,1,0:T(8,128)S(1)} %copy-done.46, ...), kind=kOutput, calls=%fused_computation.385 | convolution fusion | flops 4847812608 | bytes 11141504 | tf_op jit(solution)/shard_map/cmr,mn->crn/dot_general | solution.py:19
  729.0 16.3 %fusion.11 = bf16[96,8,1024]{2,1,0:T(8,128)(2,1)} fusion(bf16[96,8,1024]{2,1,0:T(8,128)(2,1)S(1)} %copy-done.22, f32[96,8,1024]{2,1,0:T(8,128)} %fusion.40, f32[96,512,8]{1,2,0:T(8,128)S(1)} %copy-done.30, f32[96]{0:T(128)S(1)} %copy-done.43, f32[96]{0:T(128)S(1)} %copy-done.45, f32[8,1024]{1,0:T(8,128)S(1)} %copy-done.36, f32[8,1024]{1,0:T(8,128)S(1)} %copy-done.34), kind=kOutput, calls=%fused_computation.21 | convolution fusion | flops 4847042560 | bytes 7930624 | tf_op jit(solution)/shard_map/cmr,mn->crn/dot_general | solution.py:19
  745.2 15.7 %all-reduce.9.cloned.1.call-done = (f32[8,1024]{1,0:T(8,128)}, f32[8,1024]{1,0:T(8,128)}) async-done(((f32[8,1024]{1,0:T(8,128)}, f32[8,1024]{1,0:T(8,128)}), (f32[8,1024]{1,0:T(8,128)}, f32[8,1024]{1,0:T(8,128)})) %all-reduce.9.cloned.1.call-update) | async-done | bytes 65552 | tf_op jit(solution)/shard_map/psum | solution.py:213
  761.7 4.5 fusion.1
  (220 shorter events, 224.6 us)
Async XLA Ops:
  7.2 12.5 %copy-start.31 = (bf16[96,8,1024]{2,1,0:T(8,128)(2,1)S(1)}, bf16[96,8,1024]{2,1,0:T(8,128)(2,1)}, u32[]{:S(2)}) copy-start(bf16[96,8,1024]{2,1,0:T(8,128)(2,1)} %param.9) | copy-start | bytes 4718596
  35.1 7.7 copy-start.21
  35.1 51.4 %copy-start.42 = (f32[96]{0:T(128)S(1)}, f32[96]{0:T(128)}, u32[]{:S(2)}) copy-start(f32[96]{0:T(128)} %param.11) | copy-start | bytes 1156
  35.1 51.4 %copy-start.44 = (f32[96]{0:T(128)S(1)}, f32[96]{0:T(128)}, u32[]{:S(2)}) copy-start(f32[96]{0:T(128)} %param.10) | copy-start | bytes 1156
  35.1 101.2 %all-to-all-start.2 = ((f32[1,2,96,512,8]{2,4,1,0,3:T(8,128)}), f32[1,2,96,512,8]{2,4,1,0,3:T(8,128)}, u32[]{:S(2)}, u32[]{:S(2)}) async-start(f32[1,2,96,512,8]{2,4,1,0,3:T(8,128)} %copy.146), calls=%async_computation.2 | async-start | bytes 8388608 | tf_op jit(solution)/shard_map/all_to_all | solution.py:146
  42.5 42.5 %all-reduce.11.cloned.1.call-start = ((), (), s32[]{:S(2)}) async-start(), calls=%async_computation.6 | async-start | bytes 131072 | tf_op jit(solution)/shard_map/psum | solution.py:132
  118.9 21.5 %copy-start.40 = (f32[1,2,96]{2,1,0:T(2,128)S(1)}, f32[1,2,96]{2,1,0:T(2,128)}, u32[]{:S(2)}) copy-start(f32[1,2,96]{2,1,0:T(2,128)} %param.13) | copy-start | bytes 2308
  118.9 49.4 %copy-start.41 = (f32[1,2,96]{2,1,0:T(2,128)S(1)}, f32[1,2,96]{2,1,0:T(2,128)}, u32[]{:S(2)}) copy-start(f32[1,2,96]{2,1,0:T(2,128)} %param.15) | copy-start | bytes 2308
  119.0 55.1 %copy-start.37 = (f32[1,2,96,96]{3,2,1,0:T(8,128)S(1)}, f32[1,2,96,96]{3,2,1,0:T(8,128)}, u32[]{:S(2)}) copy-start(f32[1,2,96,96]{3,2,1,0:T(8,128)} %param.12) | copy-start | bytes 221188
  119.0 61.8 %copy-start.38 = (f32[1,2,96,96]{3,2,1,0:T(8,128)S(1)}, f32[1,2,96,96]{3,2,1,0:T(8,128)}, u32[]{:S(2)}) copy-start(f32[1,2,96,96]{3,2,1,0:T(8,128)} %param.14) | copy-start | bytes 221188
  136.2 97.9 %all-to-all-start = ((f32[1,2,96,512,8]{2,4,1,0,3:T(8,128)}), f32[1,2,96,512,8]{2,4,1,0,3:T(8,128)}, u32[]{:S(2)}, u32[]{:S(2)}) async-start(f32[1,2,96,512,8]{2,4,1,0,3:T(8,128)} %copy.129), calls=%async_computation | async-start | bytes 8388608 | tf_op jit(solution)/shard_map/all_to_all | solution.py:145
  273.0 4.5 copy-start
  287.3 3.7 copy-start.10
  333.8 4.0 copy-start.25
  382.5 97.9 %all-to-all-start.3 = ((f32[32,2,96,16,8]{2,4,3,1,0:T(8,128)}), f32[32,2,96,16,8]{2,4,3,1,0:T(8,128)}, u32[]{:S(2)}, u32[]{:S(2)}) async-start(f32[32,2,96,16,8]{2,4,3,1,0:T(8,128)} %bitcast.525), calls=%async_computation.3 | async-start | bytes 8388608 | tf_op jit(solution)/shard_map/all_to_all | solution.py:196
  480.5 206.6 %all-to-all-start.1 = ((f32[32,1,2,96,16,8]{3,5,4,2,1,0:T(8,128)}), f32[32,1,2,96,16,8]{3,5,4,2,1,0:T(8,128)}, u32[]{:S(2)}, u32[]{:S(2)}) async-start(f32[32,1,2,96,16,8]{3,5,4,2,1,0:T(8,128)} %fusion.210), calls=%async_computation.1 | async-start | bytes 8388608 | tf_op jit(solution)/shard_map/all_to_all | solution.py:14
  484.7 176.5 %all-reduce.7.cloned.1.call-start = ((), (), s32[]{:S(2)}) async-start(), calls=%async_computation.4 | async-start | bytes 1179648
  484.9 5.9 copy-start.2
  484.9 5.9 copy-start.16
  490.8 3.5 copy-start.4
  501.7 3.5 copy-start.14
  505.2 3.5 copy-start.11
  517.7 243.2 %all-reduce.9.cloned.1.call-start = ((), (), s32[]{:S(2)}) async-start(), calls=%async_computation.5 | async-start | bytes 131072 | tf_op jit(solution)/shard_map/psum | solution.py:213
  697.2 15.8 %copy-start.22 = (bf16[96,8,1024]{2,1,0:T(8,128)(2,1)S(1)}, bf16[96,8,1024]{2,1,0:T(8,128)(2,1)}, u32[]{:S(2)}) copy-start(bf16[96,8,1024]{2,1,0:T(8,128)(2,1)} %param.8) | copy-start | bytes 4718596
  697.2 15.8 %copy-start.29 = (f32[96,512,8]{1,2,0:T(8,128)S(1)}, f32[96,512,8]{1,2,0:T(8,128)}, u32[]{:S(2)}) copy-start(f32[96,512,8]{1,2,0:T(8,128)} %copy.155) | copy-start | bytes 4718596
  697.2 15.8 %copy-start.32 = (bf16[96,8,1024]{2,1,0:T(8,128)(2,1)S(1)}, bf16[96,8,1024]{2,1,0:T(8,128)(2,1)}, u32[]{:S(2)}) copy-start(bf16[96,8,1024]{2,1,0:T(8,128)(2,1)} %param.9) | copy-start | bytes 4718596
  697.2 15.8 %copy-start.34 = (f32[8,1024]{1,0:T(8,128)S(1)}, f32[8,1024]{1,0:T(8,128)}, u32[]{:S(2)}) copy-start(f32[8,1024]{1,0:T(8,128)} %copy-done.33) | copy-start | bytes 98308
  697.2 15.8 %copy-start.36 = (f32[8,1024]{1,0:T(8,128)S(1)}, f32[8,1024]{1,0:T(8,128)}, u32[]{:S(2)}) copy-start(f32[8,1024]{1,0:T(8,128)} %copy-done.35) | copy-start | bytes 98308
  697.2 15.8 %copy-start.45 = (f32[96]{0:T(128)S(1)}, f32[96]{0:T(128)}, u32[]{:S(2)}) copy-start(f32[96]{0:T(128)} %param.10) | copy-start | bytes 1156
  697.2 15.8 %copy-start.46 = (f32[96,8,1024]{2,1,0:T(8,128)S(1)}, f32[96,8,1024]{2,1,0:T(8,128)}, u32[]{:S(2)}) copy-start(f32[96,8,1024]{2,1,0:T(8,128)} %fusion.38) | copy-start | bytes 9437188
  713.0 15.9 %copy-start.30 = (f32[96,512,8]{1,2,0:T(8,128)S(1)}, f32[96,512,8]{1,2,0:T(8,128)}, u32[]{:S(2)}) copy-start(f32[96,512,8]{1,2,0:T(8,128)} %copy.142) | copy-start | bytes 4718596
  713.0 15.9 %copy-start.43 = (f32[96]{0:T(128)S(1)}, f32[96]{0:T(128)}, u32[]{:S(2)}) copy-start(f32[96]{0:T(128)} %param.11) | copy-start | bytes 1156
  (22 other events, 57.3 us)
Sparse Core Ops, SparseCore 0:
  46.3 38.6 all-reduce.10
  517.8 143.3 all-reduce.6
  729.1 31.7 all-reduce.8
